TPU v7x, 32 devices: a whole 2x2x4 slice. The times are simulated.
32 devices in a mesh: groups: 2 (over y), expert: 8 (over z, core), attn: 2 (over x).
Axes of the slice: x: 2, y: 2, z: 4, core: 2. Of those that a mesh axis runs over, the one named last changes fastest.
Arguments:
- tokens: bfloat16 [512, 3584], P(('groups', 'expert')), parts along dimension 0, may hold values from -6 to 6
- gates: float32 [512, 8], P(('groups', 'expert')), parts along dimension 0, may hold values from 0.05 to 0.6
- slots: int32 [512, 8], P(('groups', 'expert')), parts along dimension 0, may hold values from 0 to 15, all different within a row; in each aligned block of 32 rows (0 to 31, 32 to 63, ...) at most 20 rows name the same one
- plan: int32 [16], P('groups'), parts along dimension 0, may hold values from 0 to 7, as said below
- gate_proj: bfloat16 [8, 3584, 1024], P('expert', None, 'attn'), may hold values from -0.09375 to 0.09375
- up_proj: bfloat16 [8, 3584, 1024], P('expert', None, 'attn'), may hold values from -0.09375 to 0.09375
- down_proj: bfloat16 [8, 3584, 1024], P('expert', None, 'attn'), may hold values from -0.1875 to 0.1875
Outputs:
- moe_out: bfloat16 [512, 3584], P(('groups', 'expert')), parts along dimension 0
There are 2 independent parts, one for each index of `groups`. A program takes and returns all parts, laid end to end along the dimension named above; an argument that names none is the same for every part. Nothing has to cross between parts.
Inputs may be any that keep to these rules, and one draw needn't show every extreme that they name: A row's 8 slots are distinct; among the 32 rows of one index of expert (aligned blocks) no slot is named more than 20 times, a bound that some block reaches. plan[d] is never d; no expert is named by more than 2 entries of plan, and some expert by exactly 2.
All inputs are finite; a program needn't handle non-finite values.
Results may differ from a plain program's by a relative error of at most 0.014.
Values may be sent and summed in bfloat16 or wider, within the bound.
No kernel may reach another device: no remote copies, remote signals or barrier semaphores. Data moves between devices by JAX's collectives and lax.ppermute only.
A program may use at most 128 MiB of HBM per device.

v0:
```python
import jax
import jax.numpy as jnp
from jax import lax
from jax.sharding import PartitionSpec as P

MULT = 2


def expert_rows(rows, w_gate, w_up, w_down):
    gate_act = jnp.dot(rows, w_gate, preferred_element_type=jnp.float32)
    up_act = jnp.dot(rows, w_up, preferred_element_type=jnp.float32)
    hidden = (jax.nn.silu(gate_act) * up_act).astype(jnp.bfloat16)
    down_out = jnp.einsum("rf,df->rd", hidden, w_down, preferred_element_type=jnp.float32)
    return down_out.astype(jnp.bfloat16)


def slot_ranks(slot_keys, key_count):
    onehot = (slot_keys[:, None] == jnp.arange(key_count, dtype=jnp.int32)[None, :]).astype(
        jnp.int32
    )
    return jnp.sum(jnp.cumsum(onehot, axis=0) * onehot, axis=1) - 1


def spread_rows(row_index, row_total, tok_count, top_count):
    matches = (
        row_index.reshape(tok_count, top_count)[None, :, :]
        == jnp.arange(row_total, dtype=jnp.int32)[:, None, None]
    )
    return jnp.sum(matches.astype(jnp.int32), axis=2).astype(jnp.bfloat16)


def body(tokens, gates, slots, plan, gate_proj, up_proj, down_proj):
    experts = lax.axis_size("expert")
    tok_count, model_width = tokens.shape
    top_count = slots.shape[1]
    capacity = max(2, min(tok_count, tok_count * top_count * 5 // (8 * experts)))
    flat_slots = slots.reshape(-1)
    device = flat_slots // 2
    slot_kind = flat_slots % 2
    owner_device = jnp.where(slot_kind == 0, device, plan[device])
    per_owner = (1 + MULT) * capacity
    position = slot_ranks(owner_device, experts)
    row_index = owner_device * per_owner + position
    row_total = experts * per_owner
    dispatch = spread_rows(row_index, row_total, tok_count, top_count)
    outgoing = jnp.dot(dispatch, tokens, preferred_element_type=jnp.float32).astype(jnp.bfloat16)
    outgoing = outgoing.reshape(experts, per_owner, model_width)
    incoming = lax.all_to_all(outgoing, "expert", split_axis=0, concat_axis=0, tiled=True)
    results = expert_rows(
        incoming.reshape(row_total, model_width), gate_proj[0], up_proj[0], down_proj[0]
    )
    results = results.reshape(experts, per_owner, model_width)
    returned = lax.all_to_all(results, "expert", split_axis=0, concat_axis=0, tiled=True).reshape(
        row_total, model_width
    )
    choice_rows = row_index.reshape(tok_count, top_count)
    partial_value = jnp.zeros((tok_count, returned.shape[1]), jnp.float32)
    for column in range(top_count):
        partial_value = (
            partial_value
            + returned[choice_rows[:, column]].astype(jnp.float32) * gates[:, column][:, None]
        )
    return lax.psum(partial_value.astype(jnp.bfloat16), "attn")


def solution(mesh):
    return jax.shard_map(
        body,
        mesh=mesh,
        in_specs=(
            P(("groups", "expert"), None),
            P(("groups", "expert"), None),
            P(("groups", "expert"), None),
            P("groups"),
            P("expert", None, "attn"),
            P("expert", None, "attn"),
            P("expert", None, "attn"),
        ),
        out_specs=P(("groups", "expert"), None),
        check_vma=False,
    )
```

profile of v0, /device:TPU:0, one launch (start us, length us, event | category | flops | bytes accessed | tf_op | source)
XLA Modules:
  0.0 286.4 jit_solution(9104749936648108147)
XLA Ops:
  6.5 0.0 copy-start
  6.5 0.8 copy.23
  7.3 0.1 reshape.197
  7.4 0.1 reshape.198
  7.5 0.1 reshape.199
  7.6 1.6 fusion.32
  9.2 4.3 %compare_select_fusion.9 = (s32[256,1]{0,1:T(1,128)S(1)}, s32[256,1]{0,1:T(1,128)S(1)}) fusion(s32[]{:T(128)} %bitcast.1, s32[]{:T(128)} %bitcast.2, s32[]{:T(128)} %bitcast.3, s32[]{:T(128)} %bitcast.4, s32[]{:T(128)} %bitcast.5, s32[]{:T(128)} %bitcast.7, s32[]{:T(128)} %bitcast.6, s32[256,1]{0,1:T(1,128)S(1)} %reshape.197), kind=kLoop, calls=%fused_computation.66 | loop fusion | flops 7680 | bytes 3100 | tf_op jit(solution)/shard_map/gather | solution.py:40
  13.6 0.7 compare_select_fusion.19
  14.2 0.1 gather.32
  14.3 0.6 reduce-window.6
  14.9 0.2 slice_reduce_fusion
  15.2 0.1 fusion.29
  15.3 0.1 sub.23
  15.4 0.2 convert_reduce_fusion
  15.6 0.0 copy-done
  15.7 2.9 convolution_convert_fusion.1
  18.5 4.6 %reshape.201 = bf16[8,60,3584]{2,1,0:T(8,128)(2,1)} reshape(bf16[480,3584]{1,0:T(8,128)(2,1)} %convolution_convert_fusion.1) | data formatting | bytes 6881280 | tf_op jit(solution)/shard_map/reshape | solution.py:47
  23.1 89.2 %all_to_all.10 = bf16[8,60,3584]{2,1,0:T(8,128)(2,1)} all-to-all(bf16[8,60,3584]{2,1,0:T(8,128)(2,1)} %reshape.201), channel_id=1, replica_groups=mesh['groups'=2,'expert'=8,'attn'=2] {'expert'}, dimensions={0} | all-to-all | bytes 6881280 | tf_op jit(solution)/shard_map/all_to_all | solution.py:48
  112.3 4.6 %reshape.202 = bf16[480,3584]{1,0:T(8,128)(2,1)} reshape(bf16[8,60,3584]{2,1,0:T(8,128)(2,1)} %all_to_all.10) | data formatting | bytes 6881280 | tf_op jit(solution)/shard_map/reshape | solution.py:50
  116.9 5.0 %fusion.3 = f32[480,512]{1,0:T(8,128)S(1)} fusion(bf16[480,3584]{1,0:T(8,128)(2,1)} %reshape.202, bf16[1,3584,512]{2,1,0:T(8,128)(2,1)} %param.11), kind=kOutput, calls=%fused_computation.13 | convolution fusion | flops 1761607680 | bytes 8093696 | tf_op jit(solution)/shard_map/dot_general | solution.py:10
  121.9 9.7 %convolution_convert_fusion = bf16[480,3584]{1,0:T(8,128)(2,1)} fusion(bf16[1,3584,512]{2,1,0:T(8,128)(2,1)} %param.13, bf16[480,3584]{1,0:T(8,128)(2,1)} %reshape.202, bf16[1,3584,512]{2,1,0:T(8,128)(2,1)} %param.12, f32[480,512]{1,0:T(8,128)S(1)} %fusion.3), kind=kOutput, calls=%fused_computation.8 | convolution fusion | flops 3526410240 | bytes 15204352 | tf_op jit(solution)/shard_map/rf,df->rd/dot_general | solution.py:13
  131.7 4.6 %reshape.203 = bf16[8,60,3584]{2,1,0:T(8,128)(2,1)} reshape(bf16[480,3584]{1,0:T(8,128)(2,1)} %convolution_convert_fusion) | data formatting | bytes 6881280 | tf_op jit(solution)/shard_map/reshape | solution.py:52
  136.3 0.0 copy-start.1
  136.3 4.6 %all-to-all-start.1 = ((bf16[8,60,3584]{2,1,0:T(8,128)(2,1)}), bf16[8,60,3584]{2,1,0:T(8,128)(2,1)}, u32[]{:S(2)}, u32[]{:S(2)}) async-start(bf16[8,60,3584]{2,1,0:T(8,128)(2,1)} %reshape.203), calls=%async_computation.1 | async-start | bytes 7340032 | tf_op jit(solution)/shard_map/all_to_all | solution.py:53
  140.9 0.2 all-reduce.2.cloned.1.call-start
  141.2 0.3 fusion.19
  141.5 0.0 copy-done.1
  141.6 82.1 %all-to-all-done.1 = bf16[8,60,3584]{2,1,0:T(8,128)(2,1)} async-done(((bf16[8,60,3584]{2,1,0:T(8,128)(2,1)}), bf16[8,60,3584]{2,1,0:T(8,128)(2,1)}, u32[]{:S(2)}, u32[]{:S(2)}) %all-to-all-start.1) | async-done | bytes 3440672 | tf_op jit(solution)/shard_map/all_to_all | solution.py:53
  223.7 4.6 %reshape.204 = bf16[480,3584]{1,0:T(8,128)(2,1)} reshape(bf16[8,60,3584]{2,1,0:T(8,128)(2,1)} %all-to-all-done.1) | data formatting | bytes 6881280 | tf_op jit(solution)/shard_map/reshape | solution.py:53
  228.3 3.3 %gather_fusion = bf16[32,3584]{1,0:T(8,128)(2,1)S(1)} fusion(bf16[480,3584]{1,0:T(8,128)(2,1)} %reshape.204, s32[1024]{0:T(1024)S(1)} %get-tuple-element.40), kind=kCustom, calls=%fused_computation | custom fusion | bytes 458880 | tf_op jit(solution)/shard_map/gather | solution.py:61
  231.6 3.3 %gather_fusion.1 = bf16[32,3584]{1,0:T(8,128)(2,1)S(1)} fusion(bf16[480,3584]{1,0:T(8,128)(2,1)} %reshape.204, s32[1024]{0:T(1024)S(1)} %get-tuple-element.39), kind=kCustom, calls=%fused_computation.1 | custom fusion | bytes 458880 | tf_op jit(solution)/shard_map/gather | solution.py:61
  234.9 3.3 %gather_fusion.2 = bf16[32,3584]{1,0:T(8,128)(2,1)S(1)} fusion(bf16[480,3584]{1,0:T(8,128)(2,1)} %reshape.204, s32[1024]{0:T(1024)S(1)} %get-tuple-element.38), kind=kCustom, calls=%fused_computation.2 | custom fusion | bytes 458880 | tf_op jit(solution)/shard_map/gather | solution.py:61
  238.3 3.3 %gather_fusion.3 = bf16[32,3584]{1,0:T(8,128)(2,1)S(1)} fusion(bf16[480,3584]{1,0:T(8,128)(2,1)} %reshape.204, s32[1024]{0:T(1024)S(1)} %get-tuple-element.37), kind=kCustom, calls=%fused_computation.3 | custom fusion | bytes 458880 | tf_op jit(solution)/shard_map/gather | solution.py:61
  241.6 3.3 %gather_fusion.4 = bf16[32,3584]{1,0:T(8,128)(2,1)S(1)} fusion(bf16[480,3584]{1,0:T(8,128)(2,1)} %reshape.204, s32[1024]{0:T(1024)S(1)} %get-tuple-element.36), kind=kCustom, calls=%fused_computation.4 | custom fusion | bytes 458880 | tf_op jit(solution)/shard_map/gather | solution.py:61
  244.9 3.3 %gather_fusion.5 = bf16[32,3584]{1,0:T(8,128)(2,1)S(1)} fusion(bf16[480,3584]{1,0:T(8,128)(2,1)} %reshape.204, s32[1024]{0:T(1024)S(1)} %get-tuple-element.35), kind=kCustom, calls=%fused_computation.5 | custom fusion | bytes 458880 | tf_op jit(solution)/shard_map/gather | solution.py:61
  248.2 3.3 %gather_fusion.6 = bf16[32,3584]{1,0:T(8,128)(2,1)S(1)} fusion(bf16[480,3584]{1,0:T(8,128)(2,1)} %reshape.204, s32[1024]{0:T(1024)S(1)} %get-tuple-element.34), kind=kCustom, calls=%fused_computation.6 | custom fusion | bytes 458880 | tf_op jit(solution)/shard_map/gather | solution.py:61
  251.6 3.3 %gather_fusion.7 = bf16[32,3584]{1,0:T(8,128)(2,1)S(1)} fusion(bf16[480,3584]{1,0:T(8,128)(2,1)} %reshape.204, s32[1024]{0:T(1024)S(1)} %get-tuple-element.33), kind=kCustom, calls=%fused_computation.7 | custom fusion | bytes 458880 | tf_op jit(solution)/shard_map/gather | solution.py:61
  254.9 1.1 add_convert_fusion
  256.0 0.0 all-reduce.2.cloned.1.call-update
  256.0 21.9 %all-reduce.2.cloned.1.call-done = bf16[32,3584]{1,0:T(8,128)(2,1)} async-done(((bf16[32,3584]{1,0:T(8,128)(2,1)}), bf16[32,3584]{1,0:T(8,128)(2,1)}) %all-reduce.2.cloned.1.call-update) | async-done | bytes 229392 | tf_op jit(solution)/shard_map/psum | solution.py:63
  277.9 1.6 copy.31
  (12 shorter events, 0.2 us)
Async XLA Ops:
  6.5 9.1 %copy-start = (bf16[32,3584]{1,0:T(8,128)(2,1)S(1)}, bf16[32,3584]{1,0:T(8,128)(2,1)}, u32[]{:S(2)}) copy-start(bf16[32,3584]{1,0:T(8,128)(2,1)} %param.7) | copy-start | bytes 688132
  136.3 5.2 %copy-start.1 = (f32[32,8]{0,1:T(8,128)S(1)}, f32[32,8]{0,1:T(8,128)}, u32[]{:S(2)}) copy-start(f32[32,8]{0,1:T(8,128)} %param.8) | copy-start | bytes 3076
  136.3 87.4 %all-to-all-start.1 = ((bf16[8,60,3584]{2,1,0:T(8,128)(2,1)}), bf16[8,60,3584]{2,1,0:T(8,128)(2,1)}, u32[]{:S(2)}, u32[]{:S(2)}) async-start(bf16[8,60,3584]{2,1,0:T(8,128)(2,1)} %reshape.203), calls=%async_computation.1 | async-start | bytes 7340032 | tf_op jit(solution)/shard_map/all_to_all | solution.py:53
  140.9 137.0 %all-reduce.2.cloned.1.call-start = ((), (), s32[]{:S(2)}) async-start(), calls=%async_computation.2 | async-start | bytes 458752 | tf_op jit(solution)/shard_map/psum | solution.py:63
Sparse Core Ops, SparseCore 0:
  256.2 21.7 all-reduce.1
where the time goes:
time: 287 us; the launch traced here: 286 us
  waiting for transfers between devices  104 us (36%)
  blocking collectives  89.2 us (31%)
  local copies, waits for them, and re-layouts  49.7 us (17%)
  matrix products  17.6 us (6%)
  between operations  13.6 us (5%)
  other arithmetic  7.44 us (3%)
  starting transfers between devices  4.85 us (2%)
    all_to_all x1, blocking collectives, body(): lax.all_to_all(outgoing, 'expert', split_axis=0, concat_axis=0, tiled=True)  89.2 us
    all_to_all x1, waiting for transfers between devices, body(): lax.all_to_all(results, 'expert', split_axis=0, concat_axis=0, tiled=True)  82.1 us
    gather x8, local copies, waits for them, and re-layouts, body(): returned[choice_rows[:, column]].astype(jnp.float32)  26.6 us
    psum x1, waiting for transfers between devices, body(): return lax.psum(partial_value.astype(jnp.bfloat16), 'attn')  21.9 us
    dot_general x1, matrix products, expert_rows(): jnp.einsum('rf,df->rd', hidden, w_down, preferred_element_type=jnp.float32)  9.75 us
  transfers between devices with their start and end apart: 2, of which 2 were waited for; matrix products, arithmetic and copies ran while one was open for 0% of the time, Pallas kernels for 0%

commit v1 on v0

--- a/solution.py
+++ b/solution.py
@@ -60,7 +60,7 @@
             partial_value
             + returned[choice_rows[:, column]].astype(jnp.float32) * gates[:, column][:, None]
         )
-    return lax.psum(partial_value.astype(jnp.bfloat16), "attn")
+    return jnp.sum(lax.all_gather(partial_value.astype(jnp.bfloat16), "attn"), axis=0)
 
 
 def solution(mesh):

time: 287 us -> 258 us (0.90)
  waiting for transfers between devices: 104 us -> 82.2 us
  between operations: 13.6 us -> 0.19 us
  blocking collectives: 89.2 us -> 96.9 us
    psum x1 -> x0, waiting for transfers between devices: 21.9 us -> none  [body(): return lax.psum(partial_value.astype(jnp.bfloat16), 'attn')]
    all_gather x0 -> x1, blocking collectives: none -> 7.72 us  [body(): lax.all_gather(partial_value.astype(jnp.bfloat16), 'attn')]
  transfers between devices with their start and end apart: 2 -> 1, of which waited for: 2 -> 1; matrix products, arithmetic and copies ran while one was open for 0% -> 0% of each run, Pallas kernels for 0% -> 0%
where the time goes in v1:
time: 258 us; the launch traced here: 257 us
  blocking collectives  96.9 us (38%)
  waiting for transfers between devices  82.2 us (32%)
  local copies, waits for them, and re-layouts  48 us (19%)
  matrix products  17.6 us (7%)
  other arithmetic  7.56 us (3%)
  starting transfers between devices  4.81 us (2%)
    all_to_all x1, blocking collectives, body(): lax.all_to_all(outgoing, 'expert', split_axis=0, concat_axis=0, tiled=True)  89.2 us
    all_to_all x1, waiting for transfers between devices, body(): lax.all_to_all(results, 'expert', split_axis=0, concat_axis=0, tiled=True)  82.2 us
    gather x8, local copies, waits for them, and re-layouts, body(): returned[choice_rows[:, column]].astype(jnp.float32)  26.6 us
    dot_general x1, matrix products, expert_rows(): jnp.einsum('rf,df->rd', hidden, w_down, preferred_element_type=jnp.float32)  9.75 us
    all_gather x1, blocking collectives, body(): lax.all_gather(partial_value.astype(jnp.bfloat16), 'attn')  7.72 us
  transfers between devices with their start and end apart: 1, of which 1 were waited for; matrix products, arithmetic and copies ran while one was open for 0% of the time, Pallas kernels for 0%

profile of v1, /device:TPU:0, one launch (start us, length us, event | category | flops | bytes accessed | tf_op | source)
XLA Modules:
  0.0 257.3 jit_solution(2097423692175895989)
XLA Ops:
  0.0 0.0 copy-start
  0.0 0.8 copy.30
  0.8 0.1 reshape.541
  0.9 0.1 reshape.542
  1.0 0.1 reshape.543
  1.1 1.6 fusion.40
  2.7 4.3 %compare_select_fusion.9 = (s32[256,1]{0,1:T(1,128)S(1)}, s32[256,1]{0,1:T(1,128)S(1)}) fusion(s32[]{:T(128)} %bitcast.1, s32[]{:T(128)} %bitcast.2, s32[]{:T(128)} %bitcast.3, s32[]{:T(128)} %bitcast.4, s32[]{:T(128)} %bitcast.5, s32[]{:T(128)} %bitcast.7, s32[]{:T(128)} %bitcast.6, s32[256,1]{0,1:T(1,128)S(1)} %reshape.541), kind=kLoop, calls=%fused_computation.81 | loop fusion | flops 7680 | bytes 3100 | tf_op jit(solution)/shard_map/gather | solution.py:40
  7.0 0.7 compare_select_fusion.19
  7.7 0.1 gather.32
  7.8 0.6 reduce-window.6
  8.4 0.2 slice_reduce_fusion
  8.7 0.1 fusion.37
  8.8 0.1 sub.23
  8.9 0.2 convert_reduce_fusion
  9.1 0.0 copy-done
  9.1 2.9 %convolution_convert_fusion.1 = bf16[480,3584]{1,0:T(8,128)(2,1)} fusion(bf16[32,3584]{1,0:T(8,128)(2,1)S(1)} %copy-done, s32[480,32]{0,1:T(8,128)S(1)} %convert_reduce_fusion), kind=kOutput, calls=%fused_computation.9 | convolution fusion | flops 111836160 | bytes 3731456 | tf_op jit(solution)/shard_map/dot_general | solution.py:46
  12.0 4.6 %reshape.545 = bf16[8,60,3584]{2,1,0:T(8,128)(2,1)} reshape(bf16[480,3584]{1,0:T(8,128)(2,1)} %convolution_convert_fusion.1) | data formatting | bytes 6881280 | tf_op jit(solution)/shard_map/reshape | solution.py:47
  16.6 89.2 %all_to_all.10 = bf16[8,60,3584]{2,1,0:T(8,128)(2,1)} all-to-all(bf16[8,60,3584]{2,1,0:T(8,128)(2,1)} %reshape.545), channel_id=1, replica_groups=mesh['groups'=2,'expert'=8,'attn'=2] {'expert'}, dimensions={0} | all-to-all | bytes 6881280 | tf_op jit(solution)/shard_map/all_to_all | solution.py:48
  105.8 4.6 %reshape.546 = bf16[480,3584]{1,0:T(8,128)(2,1)} reshape(bf16[8,60,3584]{2,1,0:T(8,128)(2,1)} %all_to_all.10) | data formatting | bytes 6881280 | tf_op jit(solution)/shard_map/reshape | solution.py:50
  110.4 5.0 %fusion.3 = f32[480,512]{1,0:T(8,128)S(1)} fusion(bf16[480,3584]{1,0:T(8,128)(2,1)} %reshape.546, bf16[1,3584,512]{2,1,0:T(8,128)(2,1)} %param.11), kind=kOutput, calls=%fused_computation.13 | convolution fusion | flops 1761607680 | bytes 8093696 | tf_op jit(solution)/shard_map/dot_general | solution.py:10
  115.4 9.7 %convolution_convert_fusion = bf16[480,3584]{1,0:T(8,128)(2,1)} fusion(bf16[1,3584,512]{2,1,0:T(8,128)(2,1)} %param.13, bf16[480,3584]{1,0:T(8,128)(2,1)} %reshape.546, bf16[1,3584,512]{2,1,0:T(8,128)(2,1)} %param.12, f32[480,512]{1,0:T(8,128)S(1)} %fusion.3), kind=kOutput, calls=%fused_computation.8 | convolution fusion | flops 3526410240 | bytes 15204352 | tf_op jit(solution)/shard_map/rf,df->rd/dot_general | solution.py:13
  125.1 4.6 %reshape.547 = bf16[8,60,3584]{2,1,0:T(8,128)(2,1)} reshape(bf16[480,3584]{1,0:T(8,128)(2,1)} %convolution_convert_fusion) | data formatting | bytes 6881280 | tf_op jit(solution)/shard_map/reshape | solution.py:52
  129.8 0.0 copy-start.1
  129.8 4.8 %all-to-all-start.1 = ((bf16[8,60,3584]{2,1,0:T(8,128)(2,1)}), bf16[8,60,3584]{2,1,0:T(8,128)(2,1)}, u32[]{:S(2)}, u32[]{:S(2)}) async-start(bf16[8,60,3584]{2,1,0:T(8,128)(2,1)} %reshape.547), calls=%async_computation.1 | async-start | bytes 7340032 | tf_op jit(solution)/shard_map/all_to_all | solution.py:53
  134.6 0.3 fusion.27
  134.9 0.0 copy-done.1
  135.0 82.2 %all-to-all-done.1 = bf16[8,60,3584]{2,1,0:T(8,128)(2,1)} async-done(((bf16[8,60,3584]{2,1,0:T(8,128)(2,1)}), bf16[8,60,3584]{2,1,0:T(8,128)(2,1)}, u32[]{:S(2)}, u32[]{:S(2)}) %all-to-all-start.1) | async-done | bytes 3440672 | tf_op jit(solution)/shard_map/all_to_all | solution.py:53
  217.1 4.6 %reshape.548 = bf16[480,3584]{1,0:T(8,128)(2,1)} reshape(bf16[8,60,3584]{2,1,0:T(8,128)(2,1)} %all-to-all-done.1) | data formatting | bytes 6881280 | tf_op jit(solution)/shard_map/reshape | solution.py:53
  221.7 3.3 %gather_fusion = bf16[32,3584]{1,0:T(8,128)(2,1)S(1)} fusion(bf16[480,3584]{1,0:T(8,128)(2,1)} %reshape.548, s32[1024]{0:T(1024)S(1)} %get-tuple-element.40), kind=kCustom, calls=%fused_computation | custom fusion | bytes 458880 | tf_op jit(solution)/shard_map/gather | solution.py:61
  225.1 3.3 %gather_fusion.1 = bf16[32,3584]{1,0:T(8,128)(2,1)S(1)} fusion(bf16[480,3584]{1,0:T(8,128)(2,1)} %reshape.548, s32[1024]{0:T(1024)S(1)} %get-tuple-element.39), kind=kCustom, calls=%fused_computation.1 | custom fusion | bytes 458880 | tf_op jit(solution)/shard_map/gather | solution.py:61
  228.4 3.3 %gather_fusion.2 = bf16[32,3584]{1,0:T(8,128)(2,1)S(1)} fusion(bf16[480,3584]{1,0:T(8,128)(2,1)} %reshape.548, s32[1024]{0:T(1024)S(1)} %get-tuple-element.38), kind=kCustom, calls=%fused_computation.2 | custom fusion | bytes 458880 | tf_op jit(solution)/shard_map/gather | solution.py:61
  231.7 3.3 %gather_fusion.3 = bf16[32,3584]{1,0:T(8,128)(2,1)S(1)} fusion(bf16[480,3584]{1,0:T(8,128)(2,1)} %reshape.548, s32[1024]{0:T(1024)S(1)} %get-tuple-element.37), kind=kCustom, calls=%fused_computation.3 | custom fusion | bytes 458880 | tf_op jit(solution)/shard_map/gather | solution.py:61
  235.0 3.3 %gather_fusion.4 = bf16[32,3584]{1,0:T(8,128)(2,1)S(1)} fusion(bf16[480,3584]{1,0:T(8,128)(2,1)} %reshape.548, s32[1024]{0:T(1024)S(1)} %get-tuple-element.36), kind=kCustom, calls=%fused_computation.4 | custom fusion | bytes 458880 | tf_op jit(solution)/shard_map/gather | solution.py:61
  238.4 3.3 %gather_fusion.5 = bf16[32,3584]{1,0:T(8,128)(2,1)S(1)} fusion(bf16[480,3584]{1,0:T(8,128)(2,1)} %reshape.548, s32[1024]{0:T(1024)S(1)} %get-tuple-element.35), kind=kCustom, calls=%fused_computation.5 | custom fusion | bytes 458880 | tf_op jit(solution)/shard_map/gather | solution.py:61
  241.7 3.3 %gather_fusion.6 = bf16[32,3584]{1,0:T(8,128)(2,1)S(1)} fusion(bf16[480,3584]{1,0:T(8,128)(2,1)} %reshape.548, s32[1024]{0:T(1024)S(1)} %get-tuple-element.34), kind=kCustom, calls=%fused_computation.6 | custom fusion | bytes 458880 | tf_op jit(solution)/shard_map/gather | solution.py:61
  245.0 3.3 %gather_fusion.7 = bf16[32,3584]{1,0:T(8,128)(2,1)S(1)} fusion(bf16[480,3584]{1,0:T(8,128)(2,1)} %reshape.548, s32[1024]{0:T(1024)S(1)} %get-tuple-element.33), kind=kCustom, calls=%fused_computation.7 | custom fusion | bytes 458880 | tf_op jit(solution)/shard_map/gather | solution.py:61
  248.4 0.4 fusion.15
  248.8 7.7 %all_gather.4 = bf16[2,32,3584]{2,1,0:T(8,128)(2,1)S(1)} all-gather(bf16[1,32,3584]{2,1,0:T(8,128)(2,1)S(1)} %fusion.15), channel_id=1, replica_groups=mesh['groups'=2,'expert'=8,'attn'=2] {'attn'}, dimensions={0}, use_global_device_ids=true | all-gather | bytes 688128 | tf_op jit(solution)/shard_map/all_gather | solution.py:63
  256.5 0.8 reduce_sum.32
  (12 shorter events, 0.2 us)
Async XLA Ops:
  0.0 9.1 %copy-start = (bf16[32,3584]{1,0:T(8,128)(2,1)S(1)}, bf16[32,3584]{1,0:T(8,128)(2,1)}, u32[]{:S(2)}) copy-start(bf16[32,3584]{1,0:T(8,128)(2,1)} %param.7) | copy-start | bytes 688132
  129.8 5.2 %copy-start.1 = (f32[32,8]{0,1:T(8,128)S(1)}, f32[32,8]{0,1:T(8,128)}, u32[]{:S(2)}) copy-start(f32[32,8]{0,1:T(8,128)} %param.8) | copy-start | bytes 3076
  129.8 87.4 %all-to-all-start.1 = ((bf16[8,60,3584]{2,1,0:T(8,128)(2,1)}), bf16[8,60,3584]{2,1,0:T(8,128)(2,1)}, u32[]{:S(2)}, u32[]{:S(2)}) async-start(bf16[8,60,3584]{2,1,0:T(8,128)(2,1)} %reshape.547), calls=%async_computation.1 | async-start | bytes 7340032 | tf_op jit(solution)/shard_map/all_to_all | solution.py:53
